TPU v7x, 256 devices: a whole 4x4x8 slice. The times are simulated.
256 devices in a mesh: ctx: 64 (over z, y, x_lo), head: 4 (over x_hi, core).
Axes of the slice: x: 4 (x_hi: 2, x_lo: 2; x = x_hi * 2 + x_lo), y: 4, z: 8, core: 2. Of those that a mesh axis runs over, the one named last changes fastest.
Arguments:
- q_nope: bfloat16 [8192, 64, 128], P('ctx', 'head'), may hold values from -6 to 6
- q_rope: bfloat16 [8192, 4096], P('ctx', 'head'), may hold values from -80 to 80
- latent: bfloat16 [8192, 576], P('ctx'), may hold values from -4 to 4
- positions: int32 [8192], P('ctx'), may hold values from 0 to 8191, each once
- w_uk: bfloat16 [64, 128, 512], P('head'), may hold values from -0.5 to 0.5
- w_uv: bfloat16 [64, 512, 128], P('head'), may hold values from -0.25 to 0.25
- w_o: bfloat16 [8192, 3584], P('head', 'ctx'), may hold values from -0.5 to 0.5
Outputs:
- projected: bfloat16 [8192, 3584], P(('ctx', 'head'))
Inputs may be any that keep to these rules, and one draw needn't show every extreme that they name: positions holds each of 0 to 8191 once.
All inputs are finite; a program needn't handle non-finite values.
Results may differ from a plain program's by a relative error of at most 0.015.
Values may be sent and summed in bfloat16 or wider, within the bound.
No kernel may reach another device: no remote copies, remote signals or barrier semaphores. Data moves between devices by JAX's collectives and lax.ppermute only.
A program may use at most 128 MiB of HBM per device.

v0:
```python
import jax
import jax.numpy as jnp
from jax import lax
from jax.sharding import PartitionSpec as P


def from_behind(x, axis, by):
    count = lax.axis_size(axis)
    return lax.ppermute(x, axis, [(i, (i + by) % count) for i in range(count)])


def local(q_nope, q_rope, latent, positions, w_uk, w_uv, w_o):
    tok_rows, heads, nope_dim = q_nope.shape
    lat_dim = w_uk.shape[2]
    rope_dim = q_rope.shape[1] // heads
    scale = (nope_dim + rope_dim) ** (-0.5)
    steps = lax.axis_size("ctx") // 4
    q_latent = jnp.einsum("thn,hnl->thl", q_nope, w_uk, preferred_element_type=jnp.float32).astype(
        jnp.bfloat16
    )
    q_rot = q_rope.reshape(tok_rows, heads, rope_dim)

    def absorb(state, keys, key_pos):
        running, total, summed = state
        scores = jnp.einsum(
            "thl,kl->thk", q_latent, keys[:, :lat_dim], preferred_element_type=jnp.float32
        )
        scores = scores + jnp.einsum(
            "thr,kr->thk", q_rot, keys[:, lat_dim:], preferred_element_type=jnp.float32
        )
        scores = scores * scale
        visible = key_pos[None, None, :] <= positions[:, None, None]
        scores = jnp.where(visible, scores, -jnp.inf)
        newest = jnp.maximum(running, jnp.max(scores, axis=-1))
        factor = jnp.exp(running - newest)
        weights = jnp.exp(scores - newest[:, :, None])
        total = total * factor + jnp.sum(weights, axis=-1)
        summed = summed * factor[:, :, None] + jnp.einsum(
            "thk,kl->thl",
            weights.astype(jnp.bfloat16),
            keys[:, :lat_dim],
            preferred_element_type=jnp.float32,
        )
        return (newest, total, summed)

    start_state = (
        jnp.full((tok_rows, heads), -jnp.inf, jnp.float32),
        jnp.zeros((tok_rows, heads), jnp.float32),
        jnp.zeros((tok_rows, heads, lat_dim), jnp.float32),
    )
    state = absorb(start_state, latent, positions)

    def turn(carry, unused):
        current, block, block_pos = carry
        block, block_pos = from_behind((block, block_pos), "ctx", 1)
        current = absorb(current, block, block_pos)
        return ((current, block, block_pos), None)

    carried, unused = lax.scan(turn, (state, latent, positions), None, length=steps - 1)
    state = carried[0]
    running, total, summed = state
    o_latent = (summed / total[:, :, None]).astype(jnp.bfloat16)
    head_out = jnp.einsum(
        "thl,hlv->thv", o_latent, w_uv, preferred_element_type=jnp.float32
    ).astype(jnp.bfloat16)
    head_out = head_out.reshape(tok_rows, heads * w_uv.shape[2])
    product = lax.dot_general(
        lax.all_gather(w_o, "ctx", axis=1, tiled=True),
        head_out,
        (((0,), (1,)), ((), ())),
        preferred_element_type=jnp.float32,
    )
    columns_first = product.astype(jnp.bfloat16)
    partial_out = columns_first.T
    summed_out = lax.psum_scatter(
        partial_out.astype(jnp.float32).astype(jnp.bfloat16),
        "head",
        scatter_dimension=0,
        tiled=True,
    )
    return summed_out


def solution(mesh):
    placed = (
        P("ctx", "head", None),
        P("ctx", "head"),
        P("ctx", None),
        P("ctx"),
        P("head", None, None),
        P("head", None, None),
        P("head", "ctx"),
    )
    return jax.shard_map(
        local, mesh=mesh, in_specs=placed, out_specs=P(("ctx", "head"), None), check_vma=False
    )
```

profile of v0, /device:TPU:1, one launch (start us, length us, event | category | flops | bytes accessed | tf_op | source)
XLA Modules:
  0.0 448.3 jit_solution(5801382140468540568)
XLA Ops:
  9.5 3.1 convert_bitcast_fusion
  12.7 3.9 copy.17
  20.0 2.7 convolution_add_fusion.1
  22.8 302.1 %while.18 = (s32[]{:T(128)}, f32[128,16]{0,1:T(8,128)S(1)}, f32[128,16]{0,1:T(8,128)S(1)}, f32[128,16,512]{2,0,1:T(8,128)}, bf16[128,576]{1,0:T(8,128)(2,1)S(1)}...) while((s32[]{:T(128)}, f32[128,16]{0,1:T(8,128)S(1)}, ...), condition=%wide.region_5.6_spmd, body=%wide.region_2.5_spmd.sunk | while | flops 575164416 | bytes 50925804 | solution.py:59
  26.1 7.8 %collective-permute-done = s32[128]{0:T(128)S(1)} collective-permute-done((s32[128]{0:T(128)S(1)}, s32[128]{0:T(128)S(1)}, u32[]{:S(2)}, u32[]{:S(2)}) %collective-permute-start) | collective-permute-done | bytes 544 | tf_op jit(solution)/shard_map/while/body/eval_jaxpr/ppermute | solution.py:9
  34.0 5.1 %collective-permute-done.1 = bf16[128,576]{1,0:T(8,128)(2,1)S(1)} collective-permute-done((bf16[128,576]{1,0:T(8,128)(2,1)S(1)}, bf16[128,576]{1,0:T(8,128)(2,1)S(1)}, u32[]{:S(2)}, u32[]{:S(2)}) %collective-permute-start.1) | collective-permute-done | bytes 147488 | tf_op jit(solution)/shard_map/while/body/eval_jaxpr/ppermute | solution.py:9
  39.4 2.4 select_reduce_fusion.2
  45.8 6.8 %collective-permute-done = s32[128]{0:T(128)S(1)} collective-permute-done((s32[128]{0:T(128)S(1)}, s32[128]{0:T(128)S(1)}, u32[]{:S(2)}, u32[]{:S(2)}) %collective-permute-start) | collective-permute-done | bytes 544 | tf_op jit(solution)/shard_map/while/body/eval_jaxpr/ppermute | solution.py:9
  52.6 5.1 %collective-permute-done.1 = bf16[128,576]{1,0:T(8,128)(2,1)S(1)} collective-permute-done((bf16[128,576]{1,0:T(8,128)(2,1)S(1)}, bf16[128,576]{1,0:T(8,128)(2,1)S(1)}, u32[]{:S(2)}, u32[]{:S(2)}) %collective-permute-start.1) | collective-permute-done | bytes 147488 | tf_op jit(solution)/shard_map/while/body/eval_jaxpr/ppermute | solution.py:9
  58.0 2.4 select_reduce_fusion.2
  64.3 6.6 %collective-permute-done = s32[128]{0:T(128)S(1)} collective-permute-done((s32[128]{0:T(128)S(1)}, s32[128]{0:T(128)S(1)}, u32[]{:S(2)}, u32[]{:S(2)}) %collective-permute-start) | collective-permute-done | bytes 544 | tf_op jit(solution)/shard_map/while/body/eval_jaxpr/ppermute | solution.py:9
  71.1 5.2 %collective-permute-done.1 = bf16[128,576]{1,0:T(8,128)(2,1)S(1)} collective-permute-done((bf16[128,576]{1,0:T(8,128)(2,1)S(1)}, bf16[128,576]{1,0:T(8,128)(2,1)S(1)}, u32[]{:S(2)}, u32[]{:S(2)}) %collective-permute-start.1) | collective-permute-done | bytes 147488 | tf_op jit(solution)/shard_map/while/body/eval_jaxpr/ppermute | solution.py:9
  76.5 2.4 select_reduce_fusion.2
  84.5 5.0 %collective-permute-done = s32[128]{0:T(128)S(1)} collective-permute-done((s32[128]{0:T(128)S(1)}, s32[128]{0:T(128)S(1)}, u32[]{:S(2)}, u32[]{:S(2)}) %collective-permute-start) | collective-permute-done | bytes 544 | tf_op jit(solution)/shard_map/while/body/eval_jaxpr/ppermute | solution.py:9
  89.6 5.7 %collective-permute-done.1 = bf16[128,576]{1,0:T(8,128)(2,1)S(1)} collective-permute-done((bf16[128,576]{1,0:T(8,128)(2,1)S(1)}, bf16[128,576]{1,0:T(8,128)(2,1)S(1)}, u32[]{:S(2)}, u32[]{:S(2)}) %collective-permute-start.1) | collective-permute-done | bytes 147488 | tf_op jit(solution)/shard_map/while/body/eval_jaxpr/ppermute | solution.py:9
  95.6 2.4 select_reduce_fusion.2
  102.0 3.4 collective-permute-start
  105.4 3.2 collective-permute-done
  108.7 7.8 %collective-permute-done.1 = bf16[128,576]{1,0:T(8,128)(2,1)S(1)} collective-permute-done((bf16[128,576]{1,0:T(8,128)(2,1)S(1)}, bf16[128,576]{1,0:T(8,128)(2,1)S(1)}, u32[]{:S(2)}, u32[]{:S(2)}) %collective-permute-start.1) | collective-permute-done | bytes 147488 | tf_op jit(solution)/shard_map/while/body/eval_jaxpr/ppermute | solution.py:9
  116.7 2.4 select_reduce_fusion.2
  123.1 3.0 collective-permute-start
  126.1 3.6 collective-permute-done
  129.8 7.5 %collective-permute-done.1 = bf16[128,576]{1,0:T(8,128)(2,1)S(1)} collective-permute-done((bf16[128,576]{1,0:T(8,128)(2,1)S(1)}, bf16[128,576]{1,0:T(8,128)(2,1)S(1)}, u32[]{:S(2)}, u32[]{:S(2)}) %collective-permute-start.1) | collective-permute-done | bytes 147488 | tf_op jit(solution)/shard_map/while/body/eval_jaxpr/ppermute | solution.py:9
  137.6 2.4 select_reduce_fusion.2
  144.0 2.3 collective-permute-start
  146.3 4.7 %collective-permute-done = s32[128]{0:T(128)S(1)} collective-permute-done((s32[128]{0:T(128)S(1)}, s32[128]{0:T(128)S(1)}, u32[]{:S(2)}, u32[]{:S(2)}) %collective-permute-start) | collective-permute-done | bytes 544 | tf_op jit(solution)/shard_map/while/body/eval_jaxpr/ppermute | solution.py:9
  151.1 6.0 %collective-permute-done.1 = bf16[128,576]{1,0:T(8,128)(2,1)S(1)} collective-permute-done((bf16[128,576]{1,0:T(8,128)(2,1)S(1)}, bf16[128,576]{1,0:T(8,128)(2,1)S(1)}, u32[]{:S(2)}, u32[]{:S(2)}) %collective-permute-start.1) | collective-permute-done | bytes 147488 | tf_op jit(solution)/shard_map/while/body/eval_jaxpr/ppermute | solution.py:9
  157.4 2.4 select_reduce_fusion.2
  163.7 2.8 collective-permute-start
  166.5 4.2 collective-permute-done
  170.8 6.4 %collective-permute-done.1 = bf16[128,576]{1,0:T(8,128)(2,1)S(1)} collective-permute-done((bf16[128,576]{1,0:T(8,128)(2,1)S(1)}, bf16[128,576]{1,0:T(8,128)(2,1)S(1)}, u32[]{:S(2)}, u32[]{:S(2)}) %collective-permute-start.1) | collective-permute-done | bytes 147488 | tf_op jit(solution)/shard_map/while/body/eval_jaxpr/ppermute | solution.py:9
  177.5 2.4 select_reduce_fusion.2
  183.8 3.1 collective-permute-start
  187.0 3.5 collective-permute-done
  190.6 7.6 %collective-permute-done.1 = bf16[128,576]{1,0:T(8,128)(2,1)S(1)} collective-permute-done((bf16[128,576]{1,0:T(8,128)(2,1)S(1)}, bf16[128,576]{1,0:T(8,128)(2,1)S(1)}, u32[]{:S(2)}, u32[]{:S(2)}) %collective-permute-start.1) | collective-permute-done | bytes 147488 | tf_op jit(solution)/shard_map/while/body/eval_jaxpr/ppermute | solution.py:9
  198.4 2.4 select_reduce_fusion.2
  204.8 2.3 collective-permute-start
  207.1 4.3 collective-permute-done
  211.5 5.8 %collective-permute-done.1 = bf16[128,576]{1,0:T(8,128)(2,1)S(1)} collective-permute-done((bf16[128,576]{1,0:T(8,128)(2,1)S(1)}, bf16[128,576]{1,0:T(8,128)(2,1)S(1)}, u32[]{:S(2)}, u32[]{:S(2)}) %collective-permute-start.1) | collective-permute-done | bytes 147488 | tf_op jit(solution)/shard_map/while/body/eval_jaxpr/ppermute | solution.py:9
  217.5 2.4 select_reduce_fusion.2
  223.9 3.2 collective-permute-start
  227.1 3.4 collective-permute-done
  230.6 7.5 %collective-permute-done.1 = bf16[128,576]{1,0:T(8,128)(2,1)S(1)} collective-permute-done((bf16[128,576]{1,0:T(8,128)(2,1)S(1)}, bf16[128,576]{1,0:T(8,128)(2,1)S(1)}, u32[]{:S(2)}, u32[]{:S(2)}) %collective-permute-start.1) | collective-permute-done | bytes 147488 | tf_op jit(solution)/shard_map/while/body/eval_jaxpr/ppermute | solution.py:9
  238.4 2.4 select_reduce_fusion.2
  244.8 2.9 collective-permute-start
  247.7 3.7 collective-permute-done
  251.5 7.4 %collective-permute-done.1 = bf16[128,576]{1,0:T(8,128)(2,1)S(1)} collective-permute-done((bf16[128,576]{1,0:T(8,128)(2,1)S(1)}, bf16[128,576]{1,0:T(8,128)(2,1)S(1)}, u32[]{:S(2)}, u32[]{:S(2)}) %collective-permute-start.1) | collective-permute-done | bytes 147488 | tf_op jit(solution)/shard_map/while/body/eval_jaxpr/ppermute | solution.py:9
  259.2 2.4 select_reduce_fusion.2
  265.5 2.3 collective-permute-start
  267.8 4.3 collective-permute-done
  272.2 6.0 %collective-permute-done.1 = bf16[128,576]{1,0:T(8,128)(2,1)S(1)} collective-permute-done((bf16[128,576]{1,0:T(8,128)(2,1)S(1)}, bf16[128,576]{1,0:T(8,128)(2,1)S(1)}, u32[]{:S(2)}, u32[]{:S(2)}) %collective-permute-start.1) | collective-permute-done | bytes 147488 | tf_op jit(solution)/shard_map/while/body/eval_jaxpr/ppermute | solution.py:9
  278.5 2.4 select_reduce_fusion.2
  284.9 3.2 collective-permute-start
  288.1 3.4 collective-permute-done
  291.6 7.6 %collective-permute-done.1 = bf16[128,576]{1,0:T(8,128)(2,1)S(1)} collective-permute-done((bf16[128,576]{1,0:T(8,128)(2,1)S(1)}, bf16[128,576]{1,0:T(8,128)(2,1)S(1)}, u32[]{:S(2)}, u32[]{:S(2)}) %collective-permute-start.1) | collective-permute-done | bytes 147488 | tf_op jit(solution)/shard_map/while/body/eval_jaxpr/ppermute | solution.py:9
  299.6 2.4 select_reduce_fusion.2
  305.9 2.3 collective-permute-start
  308.2 4.3 collective-permute-done
  312.6 5.6 %collective-permute-done.1 = bf16[128,576]{1,0:T(8,128)(2,1)S(1)} collective-permute-done((bf16[128,576]{1,0:T(8,128)(2,1)S(1)}, bf16[128,576]{1,0:T(8,128)(2,1)S(1)}, u32[]{:S(2)}, u32[]{:S(2)}) %collective-permute-start.1) | collective-permute-done | bytes 147488 | tf_op jit(solution)/shard_map/while/body/eval_jaxpr/ppermute | solution.py:9
  318.5 2.4 select_reduce_fusion.2
  324.8 4.0 fusion.12
  328.8 64.8 %all-gather.2.cloned.1.call-done = bf16[2048,3584]{0,1:T(8,128)(2,1)} async-done(((bf16[2048,56]{0,1:T(8,128)(2,1)}), bf16[2048,3584]{0,1:T(8,128)(2,1)}) %all-gather.2.cloned.1.call-update) | async-done | bytes 14680080 | tf_op jit(solution)/shard_map/all_gather | solution.py:68
  393.7 11.1 %convolution_convert_fusion = bf16[128,3584]{1,0:T(8,128)(2,1)} fusion(bf16[128,2048]{0,1:T(8,128)(2,1)S(1)} %bitcast.44, bf16[2048,3584]{0,1:T(8,128)(2,1)} %all-gather.2.cloned.1.call-done), kind=kOutput, calls=%fused_computation.17 | convolution fusion | flops 1879506944 | bytes 16121856 | tf_op jit(solution)/shard_map/dot_general | solution.py:67
  404.8 36.7 %reduce-scatter.2.cloned.1.call-done = bf16[32,3584]{1,0:T(8,128)(2,1)} async-done(((bf16[128,3584]{1,0:T(8,128)(2,1)}), bf16[32,3584]{1,0:T(8,128)(2,1)}) %reduce-scatter.2.cloned.1.call-update) | async-done | bytes 229392 | tf_op jit(solution)/shard_map/reduce_scatter | solution.py:75
  (230 shorter events, 74.8 us)
Async XLA Ops:
  6.5 3.0 copy-start
  6.5 387.1 %all-gather.2.cloned.1.call-start = ((), (), s32[]{:S(2)}) async-start(), calls=%async_computation.1 | async-start | bytes 14909440 | tf_op jit(solution)/shard_map/all_gather | solution.py:68
  7.3 434.2 %reduce-scatter.2.cloned.1.call-start = ((), (), s32[]{:S(2)}) async-start(), calls=%async_computation.2 | async-start | bytes 1146880 | tf_op jit(solution)/shard_map/reduce_scatter | solution.py:75
  9.5 7.1 %copy-start.3 = (s32[128]{0:T(128)S(1)}, s32[128]{0:T(128)}, u32[]{:S(2)}) copy-start(s32[128]{0:T(128)} %param.12) | copy-start | bytes 1540
  22.8 11.1 %collective-permute-start = (s32[128]{0:T(128)S(1)}, s32[128]{0:T(128)S(1)}, u32[]{:S(2)}, u32[]{:S(2)}) collective-permute-start(s32[128]{0:T(128)S(1)} %get-tuple-element.168), channel_id=1, source_target_pairs={{0,4},{4,8},{8,12},{12,16},{16,20},{20,24},{24,28},{28,32},{32,36}... | collective-permute-start | bytes 1544 | tf_op jit(solution)/shard_map/while/body/eval_jaxpr/ppermute | solution.py:9
  24.8 14.3 %collective-permute-start.1 = (bf16[128,576]{1,0:T(8,128)(2,1)S(1)}, bf16[128,576]{1,0:T(8,128)(2,1)S(1)}, u32[]{:S(2)}, u32[]{:S(2)}) collective-permute-start(bf16[128,576]{1,0:T(8,128)(2,1)S(1)} %get-tuple-element.167), channel_id=1, source_target_pairs={{0,4},{4,8},{8,12},{12,16},{16,20},{20,24},{24,28},{28,32},{32,36}... | collective-permute-start | bytes 442376 | tf_op jit(solution)/shard_map/while/body/eval_jaxpr/ppermute | solution.py:9
  26.1 16.0 %copy-start.1 = (f32[128,16,512]{2,0,1:T(8,128)S(1)}, f32[128,16,512]{2,0,1:T(8,128)}, u32[]{:S(2)}) copy-start(f32[128,16,512]{2,0,1:T(8,128)} %get-tuple-element.166) | copy-start | bytes 12582916 | tf_op jit(solution)/shard_map/while
  43.8 2.0 copy-start.2
  45.8 6.8 %collective-permute-start = (s32[128]{0:T(128)S(1)}, s32[128]{0:T(128)S(1)}, u32[]{:S(2)}, u32[]{:S(2)}) collective-permute-start(s32[128]{0:T(128)S(1)} %get-tuple-element.168), channel_id=1, source_target_pairs={{0,4},{4,8},{8,12},{12,16},{16,20},{20,24},{24,28},{28,32},{32,36}... | collective-permute-start | bytes 1544 | tf_op jit(solution)/shard_map/while/body/eval_jaxpr/ppermute | solution.py:9
  45.8 11.9 %collective-permute-start.1 = (bf16[128,576]{1,0:T(8,128)(2,1)S(1)}, bf16[128,576]{1,0:T(8,128)(2,1)S(1)}, u32[]{:S(2)}, u32[]{:S(2)}) collective-permute-start(bf16[128,576]{1,0:T(8,128)(2,1)S(1)} %get-tuple-element.167), channel_id=1, source_target_pairs={{0,4},{4,8},{8,12},{12,16},{16,20},{20,24},{24,28},{28,32},{32,36}... | collective-permute-start | bytes 442376 | tf_op jit(solution)/shard_map/while/body/eval_jaxpr/ppermute | solution.py:9
  45.8 14.9 %copy-start.1 = (f32[128,16,512]{2,0,1:T(8,128)S(1)}, f32[128,16,512]{2,0,1:T(8,128)}, u32[]{:S(2)}) copy-start(f32[128,16,512]{2,0,1:T(8,128)} %get-tuple-element.166) | copy-start | bytes 12582916 | tf_op jit(solution)/shard_map/while
  62.4 2.0 copy-start.2
  64.3 6.6 %collective-permute-start = (s32[128]{0:T(128)S(1)}, s32[128]{0:T(128)S(1)}, u32[]{:S(2)}, u32[]{:S(2)}) collective-permute-start(s32[128]{0:T(128)S(1)} %get-tuple-element.168), channel_id=1, source_target_pairs={{0,4},{4,8},{8,12},{12,16},{16,20},{20,24},{24,28},{28,32},{32,36}... | collective-permute-start | bytes 1544 | tf_op jit(solution)/shard_map/while/body/eval_jaxpr/ppermute | solution.py:9
  64.3 11.9 %collective-permute-start.1 = (bf16[128,576]{1,0:T(8,128)(2,1)S(1)}, bf16[128,576]{1,0:T(8,128)(2,1)S(1)}, u32[]{:S(2)}, u32[]{:S(2)}) collective-permute-start(bf16[128,576]{1,0:T(8,128)(2,1)S(1)} %get-tuple-element.167), channel_id=1, source_target_pairs={{0,4},{4,8},{8,12},{12,16},{16,20},{20,24},{24,28},{28,32},{32,36}... | collective-permute-start | bytes 442376 | tf_op jit(solution)/shard_map/while/body/eval_jaxpr/ppermute | solution.py:9
  64.3 14.9 %copy-start.1 = (f32[128,16,512]{2,0,1:T(8,128)S(1)}, f32[128,16,512]{2,0,1:T(8,128)}, u32[]{:S(2)}) copy-start(f32[128,16,512]{2,0,1:T(8,128)} %get-tuple-element.166) | copy-start | bytes 12582916 | tf_op jit(solution)/shard_map/while
  80.9 2.0 copy-start.2
  82.9 6.6 %collective-permute-start = (s32[128]{0:T(128)S(1)}, s32[128]{0:T(128)S(1)}, u32[]{:S(2)}, u32[]{:S(2)}) collective-permute-start(s32[128]{0:T(128)S(1)} %get-tuple-element.168), channel_id=1, source_target_pairs={{0,4},{4,8},{8,12},{12,16},{16,20},{20,24},{24,28},{28,32},{32,36}... | collective-permute-start | bytes 1544 | tf_op jit(solution)/shard_map/while/body/eval_jaxpr/ppermute | solution.py:9
  84.5 10.8 %collective-permute-start.1 = (bf16[128,576]{1,0:T(8,128)(2,1)S(1)}, bf16[128,576]{1,0:T(8,128)(2,1)S(1)}, u32[]{:S(2)}, u32[]{:S(2)}) collective-permute-start(bf16[128,576]{1,0:T(8,128)(2,1)S(1)} %get-tuple-element.167), channel_id=1, source_target_pairs={{0,4},{4,8},{8,12},{12,16},{16,20},{20,24},{24,28},{28,32},{32,36}... | collective-permute-start | bytes 442376 | tf_op jit(solution)/shard_map/while/body/eval_jaxpr/ppermute | solution.py:9
  84.5 13.8 %copy-start.1 = (f32[128,16,512]{2,0,1:T(8,128)S(1)}, f32[128,16,512]{2,0,1:T(8,128)}, u32[]{:S(2)}) copy-start(f32[128,16,512]{2,0,1:T(8,128)} %get-tuple-element.166) | copy-start | bytes 12582916 | tf_op jit(solution)/shard_map/while
  100.0 2.0 copy-start.2
  102.0 6.6 %collective-permute-start = (s32[128]{0:T(128)S(1)}, s32[128]{0:T(128)S(1)}, u32[]{:S(2)}, u32[]{:S(2)}) collective-permute-start(s32[128]{0:T(128)S(1)} %get-tuple-element.168), channel_id=1, source_target_pairs={{0,4},{4,8},{8,12},{12,16},{16,20},{20,24},{24,28},{28,32},{32,36}... | collective-permute-start | bytes 1544 | tf_op jit(solution)/shard_map/while/body/eval_jaxpr/ppermute | solution.py:9
  105.4 11.1 %collective-permute-start.1 = (bf16[128,576]{1,0:T(8,128)(2,1)S(1)}, bf16[128,576]{1,0:T(8,128)(2,1)S(1)}, u32[]{:S(2)}, u32[]{:S(2)}) collective-permute-start(bf16[128,576]{1,0:T(8,128)(2,1)S(1)} %get-tuple-element.167), channel_id=1, source_target_pairs={{0,4},{4,8},{8,12},{12,16},{16,20},{20,24},{24,28},{28,32},{32,36}... | collective-permute-start | bytes 442376 | tf_op jit(solution)/shard_map/while/body/eval_jaxpr/ppermute | solution.py:9
  105.4 14.1 %copy-start.1 = (f32[128,16,512]{2,0,1:T(8,128)S(1)}, f32[128,16,512]{2,0,1:T(8,128)}, u32[]{:S(2)}) copy-start(f32[128,16,512]{2,0,1:T(8,128)} %get-tuple-element.166) | copy-start | bytes 12582916 | tf_op jit(solution)/shard_map/while
  121.1 2.0 copy-start.2
  123.1 6.6 %collective-permute-start = (s32[128]{0:T(128)S(1)}, s32[128]{0:T(128)S(1)}, u32[]{:S(2)}, u32[]{:S(2)}) collective-permute-start(s32[128]{0:T(128)S(1)} %get-tuple-element.168), channel_id=1, source_target_pairs={{0,4},{4,8},{8,12},{12,16},{16,20},{20,24},{24,28},{28,32},{32,36}... | collective-permute-start | bytes 1544 | tf_op jit(solution)/shard_map/while/body/eval_jaxpr/ppermute | solution.py:9
  126.1 11.3 %collective-permute-start.1 = (bf16[128,576]{1,0:T(8,128)(2,1)S(1)}, bf16[128,576]{1,0:T(8,128)(2,1)S(1)}, u32[]{:S(2)}, u32[]{:S(2)}) collective-permute-start(bf16[128,576]{1,0:T(8,128)(2,1)S(1)} %get-tuple-element.167), channel_id=1, source_target_pairs={{0,4},{4,8},{8,12},{12,16},{16,20},{20,24},{24,28},{28,32},{32,36}... | collective-permute-start | bytes 442376 | tf_op jit(solution)/shard_map/while/body/eval_jaxpr/ppermute | solution.py:9
  126.1 14.2 %copy-start.1 = (f32[128,16,512]{2,0,1:T(8,128)S(1)}, f32[128,16,512]{2,0,1:T(8,128)}, u32[]{:S(2)}) copy-start(f32[128,16,512]{2,0,1:T(8,128)} %get-tuple-element.166) | copy-start | bytes 12582916 | tf_op jit(solution)/shard_map/while
  142.0 2.0 copy-start.2
  144.0 7.0 %collective-permute-start = (s32[128]{0:T(128)S(1)}, s32[128]{0:T(128)S(1)}, u32[]{:S(2)}, u32[]{:S(2)}) collective-permute-start(s32[128]{0:T(128)S(1)} %get-tuple-element.168), channel_id=1, source_target_pairs={{0,4},{4,8},{8,12},{12,16},{16,20},{20,24},{24,28},{28,32},{32,36}... | collective-permute-start | bytes 1544 | tf_op jit(solution)/shard_map/while/body/eval_jaxpr/ppermute | solution.py:9
  146.3 10.8 %collective-permute-start.1 = (bf16[128,576]{1,0:T(8,128)(2,1)S(1)}, bf16[128,576]{1,0:T(8,128)(2,1)S(1)}, u32[]{:S(2)}, u32[]{:S(2)}) collective-permute-start(bf16[128,576]{1,0:T(8,128)(2,1)S(1)} %get-tuple-element.167), channel_id=1, source_target_pairs={{0,4},{4,8},{8,12},{12,16},{16,20},{20,24},{24,28},{28,32},{32,36}... | collective-permute-start | bytes 442376 | tf_op jit(solution)/shard_map/while/body/eval_jaxpr/ppermute | solution.py:9
  146.3 13.8 %copy-start.1 = (f32[128,16,512]{2,0,1:T(8,128)S(1)}, f32[128,16,512]{2,0,1:T(8,128)}, u32[]{:S(2)}) copy-start(f32[128,16,512]{2,0,1:T(8,128)} %get-tuple-element.166) | copy-start | bytes 12582916 | tf_op jit(solution)/shard_map/while
  161.8 2.0 copy-start.2
  163.7 7.0 %collective-permute-start = (s32[128]{0:T(128)S(1)}, s32[128]{0:T(128)S(1)}, u32[]{:S(2)}, u32[]{:S(2)}) collective-permute-start(s32[128]{0:T(128)S(1)} %get-tuple-element.168), channel_id=1, source_target_pairs={{0,4},{4,8},{8,12},{12,16},{16,20},{20,24},{24,28},{28,32},{32,36}... | collective-permute-start | bytes 1544 | tf_op jit(solution)/shard_map/while/body/eval_jaxpr/ppermute | solution.py:9
  166.5 10.7 %collective-permute-start.1 = (bf16[128,576]{1,0:T(8,128)(2,1)S(1)}, bf16[128,576]{1,0:T(8,128)(2,1)S(1)}, u32[]{:S(2)}, u32[]{:S(2)}) collective-permute-start(bf16[128,576]{1,0:T(8,128)(2,1)S(1)} %get-tuple-element.167), channel_id=1, source_target_pairs={{0,4},{4,8},{8,12},{12,16},{16,20},{20,24},{24,28},{28,32},{32,36}... | collective-permute-start | bytes 442376 | tf_op jit(solution)/shard_map/while/body/eval_jaxpr/ppermute | solution.py:9
  166.5 13.6 %copy-start.1 = (f32[128,16,512]{2,0,1:T(8,128)S(1)}, f32[128,16,512]{2,0,1:T(8,128)}, u32[]{:S(2)}) copy-start(f32[128,16,512]{2,0,1:T(8,128)} %get-tuple-element.166) | copy-start | bytes 12582916 | tf_op jit(solution)/shard_map/while
  181.9 2.0 copy-start.2
  183.8 6.6 %collective-permute-start = (s32[128]{0:T(128)S(1)}, s32[128]{0:T(128)S(1)}, u32[]{:S(2)}, u32[]{:S(2)}) collective-permute-start(s32[128]{0:T(128)S(1)} %get-tuple-element.168), channel_id=1, source_target_pairs={{0,4},{4,8},{8,12},{12,16},{16,20},{20,24},{24,28},{28,32},{32,36}... | collective-permute-start | bytes 1544 | tf_op jit(solution)/shard_map/while/body/eval_jaxpr/ppermute | solution.py:9
  187.0 11.2 %collective-permute-start.1 = (bf16[128,576]{1,0:T(8,128)(2,1)S(1)}, bf16[128,576]{1,0:T(8,128)(2,1)S(1)}, u32[]{:S(2)}, u32[]{:S(2)}) collective-permute-start(bf16[128,576]{1,0:T(8,128)(2,1)S(1)} %get-tuple-element.167), channel_id=1, source_target_pairs={{0,4},{4,8},{8,12},{12,16},{16,20},{20,24},{24,28},{28,32},{32,36}... | collective-permute-start | bytes 442376 | tf_op jit(solution)/shard_map/while/body/eval_jaxpr/ppermute | solution.py:9
  187.0 14.1 %copy-start.1 = (f32[128,16,512]{2,0,1:T(8,128)S(1)}, f32[128,16,512]{2,0,1:T(8,128)}, u32[]{:S(2)}) copy-start(f32[128,16,512]{2,0,1:T(8,128)} %get-tuple-element.166) | copy-start | bytes 12582916 | tf_op jit(solution)/shard_map/while
  202.8 2.0 copy-start.2
  204.8 6.6 %collective-permute-start = (s32[128]{0:T(128)S(1)}, s32[128]{0:T(128)S(1)}, u32[]{:S(2)}, u32[]{:S(2)}) collective-permute-start(s32[128]{0:T(128)S(1)} %get-tuple-element.168), channel_id=1, source_target_pairs={{0,4},{4,8},{8,12},{12,16},{16,20},{20,24},{24,28},{28,32},{32,36}... | collective-permute-start | bytes 1544 | tf_op jit(solution)/shard_map/while/body/eval_jaxpr/ppermute | solution.py:9
  207.1 10.2 %collective-permute-start.1 = (bf16[128,576]{1,0:T(8,128)(2,1)S(1)}, bf16[128,576]{1,0:T(8,128)(2,1)S(1)}, u32[]{:S(2)}, u32[]{:S(2)}) collective-permute-start(bf16[128,576]{1,0:T(8,128)(2,1)S(1)} %get-tuple-element.167), channel_id=1, source_target_pairs={{0,4},{4,8},{8,12},{12,16},{16,20},{20,24},{24,28},{28,32},{32,36}... | collective-permute-start | bytes 442376 | tf_op jit(solution)/shard_map/while/body/eval_jaxpr/ppermute | solution.py:9
  207.1 13.1 %copy-start.1 = (f32[128,16,512]{2,0,1:T(8,128)S(1)}, f32[128,16,512]{2,0,1:T(8,128)}, u32[]{:S(2)}) copy-start(f32[128,16,512]{2,0,1:T(8,128)} %get-tuple-element.166) | copy-start | bytes 12582916 | tf_op jit(solution)/shard_map/while
  221.9 2.0 copy-start.2
  223.9 6.6 %collective-permute-start = (s32[128]{0:T(128)S(1)}, s32[128]{0:T(128)S(1)}, u32[]{:S(2)}, u32[]{:S(2)}) collective-permute-start(s32[128]{0:T(128)S(1)} %get-tuple-element.168), channel_id=1, source_target_pairs={{0,4},{4,8},{8,12},{12,16},{16,20},{20,24},{24,28},{28,32},{32,36}... | collective-permute-start | bytes 1544 | tf_op jit(solution)/shard_map/while/body/eval_jaxpr/ppermute | solution.py:9
  227.0 11.1 %collective-permute-start.1 = (bf16[128,576]{1,0:T(8,128)(2,1)S(1)}, bf16[128,576]{1,0:T(8,128)(2,1)S(1)}, u32[]{:S(2)}, u32[]{:S(2)}) collective-permute-start(bf16[128,576]{1,0:T(8,128)(2,1)S(1)} %get-tuple-element.167), channel_id=1, source_target_pairs={{0,4},{4,8},{8,12},{12,16},{16,20},{20,24},{24,28},{28,32},{32,36}... | collective-permute-start | bytes 442376 | tf_op jit(solution)/shard_map/while/body/eval_jaxpr/ppermute | solution.py:9
  227.1 14.0 %copy-start.1 = (f32[128,16,512]{2,0,1:T(8,128)S(1)}, f32[128,16,512]{2,0,1:T(8,128)}, u32[]{:S(2)}) copy-start(f32[128,16,512]{2,0,1:T(8,128)} %get-tuple-element.166) | copy-start | bytes 12582916 | tf_op jit(solution)/shard_map/while
  242.8 2.0 copy-start.2
  244.8 6.6 %collective-permute-start = (s32[128]{0:T(128)S(1)}, s32[128]{0:T(128)S(1)}, u32[]{:S(2)}, u32[]{:S(2)}) collective-permute-start(s32[128]{0:T(128)S(1)} %get-tuple-element.168), channel_id=1, source_target_pairs={{0,4},{4,8},{8,12},{12,16},{16,20},{20,24},{24,28},{28,32},{32,36}... | collective-permute-start | bytes 1544 | tf_op jit(solution)/shard_map/while/body/eval_jaxpr/ppermute | solution.py:9
  247.7 11.2 %collective-permute-start.1 = (bf16[128,576]{1,0:T(8,128)(2,1)S(1)}, bf16[128,576]{1,0:T(8,128)(2,1)S(1)}, u32[]{:S(2)}, u32[]{:S(2)}) collective-permute-start(bf16[128,576]{1,0:T(8,128)(2,1)S(1)} %get-tuple-element.167), channel_id=1, source_target_pairs={{0,4},{4,8},{8,12},{12,16},{16,20},{20,24},{24,28},{28,32},{32,36}... | collective-permute-start | bytes 442376 | tf_op jit(solution)/shard_map/while/body/eval_jaxpr/ppermute | solution.py:9
  247.7 14.1 %copy-start.1 = (f32[128,16,512]{2,0,1:T(8,128)S(1)}, f32[128,16,512]{2,0,1:T(8,128)}, u32[]{:S(2)}) copy-start(f32[128,16,512]{2,0,1:T(8,128)} %get-tuple-element.166) | copy-start | bytes 12582916 | tf_op jit(solution)/shard_map/while
  263.5 2.0 copy-start.2
  265.5 6.6 %collective-permute-start = (s32[128]{0:T(128)S(1)}, s32[128]{0:T(128)S(1)}, u32[]{:S(2)}, u32[]{:S(2)}) collective-permute-start(s32[128]{0:T(128)S(1)} %get-tuple-element.168), channel_id=1, source_target_pairs={{0,4},{4,8},{8,12},{12,16},{16,20},{20,24},{24,28},{28,32},{32,36}... | collective-permute-start | bytes 1544 | tf_op jit(solution)/shard_map/while/body/eval_jaxpr/ppermute | solution.py:9
  267.8 10.5 %collective-permute-start.1 = (bf16[128,576]{1,0:T(8,128)(2,1)S(1)}, bf16[128,576]{1,0:T(8,128)(2,1)S(1)}, u32[]{:S(2)}, u32[]{:S(2)}) collective-permute-start(bf16[128,576]{1,0:T(8,128)(2,1)S(1)} %get-tuple-element.167), channel_id=1, source_target_pairs={{0,4},{4,8},{8,12},{12,16},{16,20},{20,24},{24,28},{28,32},{32,36}... | collective-permute-start | bytes 442376 | tf_op jit(solution)/shard_map/while/body/eval_jaxpr/ppermute | solution.py:9
  267.8 13.4 %copy-start.1 = (f32[128,16,512]{2,0,1:T(8,128)S(1)}, f32[128,16,512]{2,0,1:T(8,128)}, u32[]{:S(2)}) copy-start(f32[128,16,512]{2,0,1:T(8,128)} %get-tuple-element.166) | copy-start | bytes 12582916 | tf_op jit(solution)/shard_map/while
  282.9 2.0 copy-start.2
  284.9 6.6 %collective-permute-start = (s32[128]{0:T(128)S(1)}, s32[128]{0:T(128)S(1)}, u32[]{:S(2)}, u32[]{:S(2)}) collective-permute-start(s32[128]{0:T(128)S(1)} %get-tuple-element.168), channel_id=1, source_target_pairs={{0,4},{4,8},{8,12},{12,16},{16,20},{20,24},{24,28},{28,32},{32,36}... | collective-permute-start | bytes 1544 | tf_op jit(solution)/shard_map/while/body/eval_jaxpr/ppermute | solution.py:9
  288.1 11.2 %collective-permute-start.1 = (bf16[128,576]{1,0:T(8,128)(2,1)S(1)}, bf16[128,576]{1,0:T(8,128)(2,1)S(1)}, u32[]{:S(2)}, u32[]{:S(2)}) collective-permute-start(bf16[128,576]{1,0:T(8,128)(2,1)S(1)} %get-tuple-element.167), channel_id=1, source_target_pairs={{0,4},{4,8},{8,12},{12,16},{16,20},{20,24},{24,28},{28,32},{32,36}... | collective-permute-start | bytes 442376 | tf_op jit(solution)/shard_map/while/body/eval_jaxpr/ppermute | solution.py:9
  288.1 14.1 %copy-start.1 = (f32[128,16,512]{2,0,1:T(8,128)S(1)}, f32[128,16,512]{2,0,1:T(8,128)}, u32[]{:S(2)}) copy-start(f32[128,16,512]{2,0,1:T(8,128)} %get-tuple-element.166) | copy-start | bytes 12582916 | tf_op jit(solution)/shard_map/while
  303.9 2.0 copy-start.2
  305.9 6.6 %collective-permute-start = (s32[128]{0:T(128)S(1)}, s32[128]{0:T(128)S(1)}, u32[]{:S(2)}, u32[]{:S(2)}) collective-permute-start(s32[128]{0:T(128)S(1)} %get-tuple-element.168), channel_id=1, source_target_pairs={{0,4},{4,8},{8,12},{12,16},{16,20},{20,24},{24,28},{28,32},{32,36}... | collective-permute-start | bytes 1544 | tf_op jit(solution)/shard_map/while/body/eval_jaxpr/ppermute | solution.py:9
  308.2 10.0 %collective-permute-start.1 = (bf16[128,576]{1,0:T(8,128)(2,1)S(1)}, bf16[128,576]{1,0:T(8,128)(2,1)S(1)}, u32[]{:S(2)}, u32[]{:S(2)}) collective-permute-start(bf16[128,576]{1,0:T(8,128)(2,1)S(1)} %get-tuple-element.167), channel_id=1, source_target_pairs={{0,4},{4,8},{8,12},{12,16},{16,20},{20,24},{24,28},{28,32},{32,36}... | collective-permute-start | bytes 442376 | tf_op jit(solution)/shard_map/while/body/eval_jaxpr/ppermute | solution.py:9
  308.2 13.0 %copy-start.1 = (f32[128,16,512]{2,0,1:T(8,128)S(1)}, f32[128,16,512]{2,0,1:T(8,128)}, u32[]{:S(2)}) copy-start(f32[128,16,512]{2,0,1:T(8,128)} %get-tuple-element.166) | copy-start | bytes 12582916 | tf_op jit(solution)/shard_map/while
  322.9 2.0 copy-start.2
Sparse Core Ops, SparseCore 0:
  9.1 384.5 all-gather.1
  404.9 36.5 reduce-scatter.1
where the time goes:
time: 449 us; the launch traced here: 448 us
  waiting for transfers between devices  267 us (59%)
  matrix products  89.5 us (20%)
  starting transfers between devices  36.2 us (8%)
  local copies, waits for them, and re-layouts  35.8 us (8%)
  between operations  13.5 us (3%)
  other arithmetic  4.66 us (1%)
    ppermute x30, waiting for transfers between devices, from_behind(): return lax.ppermute(x, axis, [(i, (i + by) % count) for i in range(count)])  165 us
    all_gather x1, waiting for transfers between devices, local(): lax.all_gather(w_o, 'ctx', axis=1, tiled=True)  64.8 us
    dot_general x16, matrix products, absorb(): jnp.einsum('thl,kl->thk', q_latent, keys[:, :lat_dim], preferred_element_...  38.4 us
    reduce_scatter x1, waiting for transfers between devices, local(): lax.psum_scatter(partial_out.astype(jnp.float32).astype(jnp.bfloat16), 'h...  36.7 us
    ppermute x30, starting transfers between devices, from_behind(): return lax.ppermute(x, axis, [(i, (i + by) % count) for i in range(count)])  36.2 us
    while x105, local copies, waits for them, and re-layouts  29.7 us
    dot_general x16, matrix products, absorb(): jnp.einsum('thk,kl->thl', weights.astype(jnp.bfloat16), keys[:, :lat_dim]...  27.8 us
    dot_general x1, matrix products, local(): lax.dot_general(lax.all_gather(w_o, 'ctx', axis=1, tiled=True), head_out,...  11.1 us
  transfers between devices with their start and end apart: 32, of which 32 were waited for; matrix products, arithmetic and copies ran while one was open for 20% of the time, Pallas kernels for 0%

commit v1 on v0

--- a/solution.py
+++ b/solution.py
@@ -2,6 +2,11 @@
 import jax.numpy as jnp
 from jax import lax
 from jax.sharding import PartitionSpec as P
+
+
+def swapped_in(value, mesh_axis, along):
+    stack = jnp.stack([value] * lax.axis_size(mesh_axis))
+    return jnp.concatenate(lax.all_to_all(stack, mesh_axis, 0, 0), axis=along)
 
 
 def from_behind(x, axis, by):
@@ -65,7 +70,7 @@
     ).astype(jnp.bfloat16)
     head_out = head_out.reshape(tok_rows, heads * w_uv.shape[2])
     product = lax.dot_general(
-        lax.all_gather(w_o, "ctx", axis=1, tiled=True),
+        swapped_in(w_o, "ctx", 1),
         head_out,
         (((0,), (1,)), ((), ())),
         preferred_element_type=jnp.float32,

time: 449 us -> 644 us (1.43)
  waiting for transfers between devices: 267 us -> 478 us
  starting transfers between devices: 36.2 us -> 16.2 us
    ppermute x30, waiting for transfers between devices: 165 us -> 420 us  [from_behind(): return lax.ppermute(x, axis, [(i, (i + by) % count) for i in range(count)])]
    all_gather x1 -> x0, waiting for transfers between devices: 64.8 us -> none  [local(): lax.all_gather(w_o, 'ctx', axis=1, tiled=True)]
    ppermute x30, starting transfers between devices: 36.2 us -> 2.2 us  [from_behind(): return lax.ppermute(x, axis, [(i, (i + by) % count) for i in range(count)])]
    reduce_scatter x1, waiting for transfers between devices: 36.7 us -> 57.5 us  [local(): lax.psum_scatter(partial_out.astype(jnp.float32).astype(jnp.bfloat16), 'h...]
    all_to_all x0 -> x1, starting transfers between devices: none -> 13.9 us  [swapped_in(): return jnp.concatenate(lax.all_to_all(stack, mesh_axis, 0, 0), axis=along)]
    another operation x0 -> x1, local copies, waits for them, and re-layouts: none -> 8.13 us  [swapped_in(): stack = jnp.stack([value] * lax.axis_size(mesh_axis))]
  transfers between devices with their start and end apart: 32 -> 32, of which waited for: 32 -> 31; matrix products, arithmetic and copies ran while one was open for 20% -> 13% of each run, Pallas kernels for 0% -> 0%
where the time goes in v1:
time: 644 us; the launch traced here: 643 us
  waiting for transfers between devices  478 us (74%)
  matrix products  87.7 us (14%)
  local copies, waits for them, and re-layouts  41.7 us (6%)
  starting transfers between devices  16.2 us (3%)
  between operations  13.5 us (2%)
    ppermute x30, waiting for transfers between devices, from_behind(): return lax.ppermute(x, axis, [(i, (i + by) % count) for i in range(count)])  420 us
    reduce_scatter x1, waiting for transfers between devices, local(): lax.psum_scatter(partial_out.astype(jnp.float32).astype(jnp.bfloat16), 'h...  57.5 us
    dot_general x16, matrix products, absorb(): jnp.einsum('thl,kl->thk', q_latent, keys[:, :lat_dim], preferred_element_...  38.3 us
    while x105, local copies, waits for them, and re-layouts  29.3 us
    dot_general x16, matrix products, absorb(): jnp.einsum('thk,kl->thl', weights.astype(jnp.bfloat16), keys[:, :lat_dim]...  27.8 us
    all_to_all x1, starting transfers between devices, swapped_in(): return jnp.concatenate(lax.all_to_all(stack, mesh_axis, 0, 0), axis=along)  13.9 us
  transfers between devices with their start and end apart: 32, of which 31 were waited for; matrix products, arithmetic and copies ran while one was open for 13% of the time, Pallas kernels for 0%

profile of v1, /device:TPU:1, one launch (start us, length us, event | category | flops | bytes accessed | tf_op | source)
XLA Modules:
  0.0 643.1 jit_solution(9916036308610209253)
XLA Ops:
  6.5 8.1 %stack.2 = bf16[64,2048,56]{1,2,0:T(8,128)(2,1)} broadcast(bf16[2048,56]{0,1:T(8,128)(2,1)} %param.15), dimensions={1,2} | broadcast | bytes 14909440 | tf_op jit(solution)/shard_map/stack | solution.py:8
  14.7 13.9 %all-to-all-start = ((bf16[64,2048,56]{1,2,0:T(8,128)(2,1)}), bf16[64,2048,56]{1,2,0:T(8,128)(2,1)}, u32[]{:S(2)}, u32[]{:S(2)}) async-start(bf16[64,2048,56]{1,2,0:T(8,128)(2,1)} %stack.2), calls=%async_computation | async-start | bytes 29360128 | tf_op jit(solution)/shard_map/all_to_all | solution.py:9
  29.1 2.1 convert_bitcast_fusion
  31.2 3.9 copy.29
  35.5 2.1 fusion.22
  37.9 2.7 convolution_add_fusion.1
  40.6 523.1 %while.18 = (s32[]{:T(128)}, f32[128,16]{0,1:T(8,128)S(1)}, f32[128,16]{0,1:T(8,128)S(1)}, f32[128,16,512]{2,0,1:T(8,128)}, bf16[128,576]{1,0:T(8,128)(2,1)S(1)}...) while((s32[]{:T(128)}, f32[128,16]{0,1:T(8,128)S(1)}, ...), condition=%wide.region_5.6_spmd, body=%wide.region_2.5_spmd.sunk | while | flops 575164416 | bytes 50925804 | solution.py:64
  42.7 286.5 %collective-permute-done = s32[128]{0:T(128)S(1)} collective-permute-done((s32[128]{0:T(128)S(1)}, s32[128]{0:T(128)S(1)}, u32[]{:S(2)}, u32[]{:S(2)}) %collective-permute-start) | collective-permute-done | bytes 544 | tf_op jit(solution)/shard_map/while/body/eval_jaxpr/ppermute | solution.py:14
  329.3 10.4 %collective-permute-done.1 = bf16[128,576]{1,0:T(8,128)(2,1)S(1)} collective-permute-done((bf16[128,576]{1,0:T(8,128)(2,1)S(1)}, bf16[128,576]{1,0:T(8,128)(2,1)S(1)}, u32[]{:S(2)}, u32[]{:S(2)}) %collective-permute-start.1) | collective-permute-done | bytes 147488 | tf_op jit(solution)/shard_map/while/body/eval_jaxpr/ppermute | solution.py:14
  340.0 2.4 select_reduce_fusion.2
  344.4 1.9 copy-done.2
  346.4 6.6 %collective-permute-done = s32[128]{0:T(128)S(1)} collective-permute-done((s32[128]{0:T(128)S(1)}, s32[128]{0:T(128)S(1)}, u32[]{:S(2)}, u32[]{:S(2)}) %collective-permute-start) | collective-permute-done | bytes 544 | tf_op jit(solution)/shard_map/while/body/eval_jaxpr/ppermute | solution.py:14
  353.1 5.5 collective-permute-done.1
  358.9 2.4 select_reduce_fusion.2
  363.2 1.9 copy-done.2
  365.2 6.6 %collective-permute-done = s32[128]{0:T(128)S(1)} collective-permute-done((s32[128]{0:T(128)S(1)}, s32[128]{0:T(128)S(1)}, u32[]{:S(2)}, u32[]{:S(2)}) %collective-permute-start) | collective-permute-done | bytes 544 | tf_op jit(solution)/shard_map/while/body/eval_jaxpr/ppermute | solution.py:14
  371.9 1.7 collective-permute-done.1
  373.9 2.4 select_reduce_fusion.2
  378.2 1.9 copy-done.2
  380.2 6.6 %collective-permute-done = s32[128]{0:T(128)S(1)} collective-permute-done((s32[128]{0:T(128)S(1)}, s32[128]{0:T(128)S(1)}, u32[]{:S(2)}, u32[]{:S(2)}) %collective-permute-start) | collective-permute-done | bytes 544 | tf_op jit(solution)/shard_map/while/body/eval_jaxpr/ppermute | solution.py:14
  386.9 1.7 collective-permute-done.1
  388.9 2.4 select_reduce_fusion.2
  393.2 1.9 copy-done.2
  395.2 6.6 %collective-permute-done = s32[128]{0:T(128)S(1)} collective-permute-done((s32[128]{0:T(128)S(1)}, s32[128]{0:T(128)S(1)}, u32[]{:S(2)}, u32[]{:S(2)}) %collective-permute-start) | collective-permute-done | bytes 544 | tf_op jit(solution)/shard_map/while/body/eval_jaxpr/ppermute | solution.py:14
  401.9 1.7 collective-permute-done.1
  403.9 2.4 select_reduce_fusion.2
  408.3 1.9 copy-done.2
  410.2 6.6 %collective-permute-done = s32[128]{0:T(128)S(1)} collective-permute-done((s32[128]{0:T(128)S(1)}, s32[128]{0:T(128)S(1)}, u32[]{:S(2)}, u32[]{:S(2)}) %collective-permute-start) | collective-permute-done | bytes 544 | tf_op jit(solution)/shard_map/while/body/eval_jaxpr/ppermute | solution.py:14
  418.9 2.4 select_reduce_fusion.2
  423.3 1.9 copy-done.2
  425.2 6.6 %collective-permute-done = s32[128]{0:T(128)S(1)} collective-permute-done((s32[128]{0:T(128)S(1)}, s32[128]{0:T(128)S(1)}, u32[]{:S(2)}, u32[]{:S(2)}) %collective-permute-start) | collective-permute-done | bytes 544 | tf_op jit(solution)/shard_map/while/body/eval_jaxpr/ppermute | solution.py:14
  433.9 2.4 select_reduce_fusion.2
  438.3 1.9 copy-done.2
  440.2 6.6 %collective-permute-done = s32[128]{0:T(128)S(1)} collective-permute-done((s32[128]{0:T(128)S(1)}, s32[128]{0:T(128)S(1)}, u32[]{:S(2)}, u32[]{:S(2)}) %collective-permute-start) | collective-permute-done | bytes 544 | tf_op jit(solution)/shard_map/while/body/eval_jaxpr/ppermute | solution.py:14
  446.9 1.7 collective-permute-done.1
  448.9 2.4 select_reduce_fusion.2
  453.3 1.9 copy-done.2
  455.2 6.6 %collective-permute-done = s32[128]{0:T(128)S(1)} collective-permute-done((s32[128]{0:T(128)S(1)}, s32[128]{0:T(128)S(1)}, u32[]{:S(2)}, u32[]{:S(2)}) %collective-permute-start) | collective-permute-done | bytes 544 | tf_op jit(solution)/shard_map/while/body/eval_jaxpr/ppermute | solution.py:14
  463.9 2.4 select_reduce_fusion.2
  468.3 1.9 copy-done.2
  470.2 6.6 %collective-permute-done = s32[128]{0:T(128)S(1)} collective-permute-done((s32[128]{0:T(128)S(1)}, s32[128]{0:T(128)S(1)}, u32[]{:S(2)}, u32[]{:S(2)}) %collective-permute-start) | collective-permute-done | bytes 544 | tf_op jit(solution)/shard_map/while/body/eval_jaxpr/ppermute | solution.py:14
  478.9 2.4 select_reduce_fusion.2
  483.3 1.9 copy-done.2
  485.2 6.6 %collective-permute-done = s32[128]{0:T(128)S(1)} collective-permute-done((s32[128]{0:T(128)S(1)}, s32[128]{0:T(128)S(1)}, u32[]{:S(2)}, u32[]{:S(2)}) %collective-permute-start) | collective-permute-done | bytes 544 | tf_op jit(solution)/shard_map/while/body/eval_jaxpr/ppermute | solution.py:14
  493.9 2.4 select_reduce_fusion.2
  498.3 1.9 copy-done.2
  500.2 6.8 %collective-permute-done = s32[128]{0:T(128)S(1)} collective-permute-done((s32[128]{0:T(128)S(1)}, s32[128]{0:T(128)S(1)}, u32[]{:S(2)}, u32[]{:S(2)}) %collective-permute-start) | collective-permute-done | bytes 544 | tf_op jit(solution)/shard_map/while/body/eval_jaxpr/ppermute | solution.py:14
  508.9 2.4 select_reduce_fusion.2
  513.3 1.9 copy-done.2
  515.2 6.9 %collective-permute-done = s32[128]{0:T(128)S(1)} collective-permute-done((s32[128]{0:T(128)S(1)}, s32[128]{0:T(128)S(1)}, u32[]{:S(2)}, u32[]{:S(2)}) %collective-permute-start) | collective-permute-done | bytes 544 | tf_op jit(solution)/shard_map/while/body/eval_jaxpr/ppermute | solution.py:14
  522.3 2.4 collective-permute-done.1
  524.9 2.4 select_reduce_fusion.2
  529.3 1.9 copy-done.2
  531.3 6.6 %collective-permute-done = s32[128]{0:T(128)S(1)} collective-permute-done((s32[128]{0:T(128)S(1)}, s32[128]{0:T(128)S(1)}, u32[]{:S(2)}, u32[]{:S(2)}) %collective-permute-start) | collective-permute-done | bytes 544 | tf_op jit(solution)/shard_map/while/body/eval_jaxpr/ppermute | solution.py:14
  538.0 3.3 collective-permute-done.1
  541.6 2.4 select_reduce_fusion.2
  545.9 1.9 copy-done.2
  547.9 6.6 %collective-permute-done = s32[128]{0:T(128)S(1)} collective-permute-done((s32[128]{0:T(128)S(1)}, s32[128]{0:T(128)S(1)}, u32[]{:S(2)}, u32[]{:S(2)}) %collective-permute-start) | collective-permute-done | bytes 544 | tf_op jit(solution)/shard_map/while/body/eval_jaxpr/ppermute | solution.py:14
  554.6 2.4 collective-permute-done.1
  557.3 2.4 select_reduce_fusion.2
  561.7 1.9 copy-done.2
  563.6 4.0 fusion.12
  567.6 11.1 %convolution_convert_fusion = bf16[128,3584]{1,0:T(8,128)(2,1)} fusion(bf16[128,2048]{0,1:T(8,128)(2,1)S(1)} %bitcast.47, bf16[2048,3584]{0,1:T(8,128)(2,1)} %bitcast.9), kind=kOutput, calls=%fused_computation.17 | convolution fusion | flops 1879506944 | bytes 16121856 | tf_op jit(solution)/shard_map/dot_general | solution.py:72
  578.8 57.5 %reduce-scatter.2.cloned.1.call-done = bf16[32,3584]{1,0:T(8,128)(2,1)} async-done(((bf16[128,3584]{1,0:T(8,128)(2,1)}), bf16[32,3584]{1,0:T(8,128)(2,1)}) %reduce-scatter.2.cloned.1.call-update) | async-done | bytes 229392 | tf_op jit(solution)/shard_map/reduce_scatter | solution.py:80
  (236 shorter events, 47.1 us)
Async XLA Ops:
  6.5 22.5 %copy-start = (bf16[16,128,512]{2,1,0:T(8,128)(2,1)S(1)}, bf16[16,128,512]{2,1,0:T(8,128)(2,1)}, u32[]{:S(2)}) copy-start(bf16[16,128,512]{2,1,0:T(8,128)(2,1)} %param.13) | copy-start | bytes 6291460
  14.7 14.0 %copy-start.6 = (s32[128]{0:T(128)S(1)}, s32[128]{0:T(128)}, u32[]{:S(2)}) copy-start(s32[128]{0:T(128)} %param.12) | copy-start | bytes 1540
  14.7 14.0 %copy-start.5 = (bf16[128,576]{0,1:T(8,128)(2,1)S(1)}, bf16[128,576]{0,1:T(8,128)(2,1)}, u32[]{:S(2)}) copy-start(bf16[128,576]{0,1:T(8,128)(2,1)} %param.11) | copy-start | bytes 442372
  14.7 14.2 %copy-start.4 = (bf16[128,1024]{1,0:T(8,128)(2,1)S(1)}, bf16[128,1024]{1,0:T(8,128)(2,1)}, u32[]{:S(2)}) copy-start(bf16[128,1024]{1,0:T(8,128)(2,1)} %param.10) | copy-start | bytes 786436
  14.7 14.4 %copy-start.3 = (bf16[128,16,128]{2,1,0:T(8,128)(2,1)S(1)}, bf16[128,16,128]{2,1,0:T(8,128)(2,1)}, u32[]{:S(2)}) copy-start(bf16[128,16,128]{2,1,0:T(8,128)(2,1)} %param.9) | copy-start | bytes 1572868
  14.7 552.9 %all-to-all-start = ((bf16[64,2048,56]{1,2,0:T(8,128)(2,1)}), bf16[64,2048,56]{1,2,0:T(8,128)(2,1)}, u32[]{:S(2)}, u32[]{:S(2)}) async-start(bf16[64,2048,56]{1,2,0:T(8,128)(2,1)} %stack.2), calls=%async_computation | async-start | bytes 29360128 | tf_op jit(solution)/shard_map/all_to_all | solution.py:9
  28.6 607.6 %reduce-scatter.2.cloned.1.call-start = ((), (), s32[]{:S(2)}) async-start(), calls=%async_computation.2 | async-start | bytes 1146880 | tf_op jit(solution)/shard_map/reduce_scatter | solution.py:80
  40.6 288.7 %collective-permute-start = (s32[128]{0:T(128)S(1)}, s32[128]{0:T(128)S(1)}, u32[]{:S(2)}, u32[]{:S(2)}) collective-permute-start(s32[128]{0:T(128)S(1)} %get-tuple-element.177), channel_id=1, source_target_pairs={{0,4},{4,8},{8,12},{12,16},{16,20},{20,24},{24,28},{28,32},{32,36}... | collective-permute-start | bytes 1544 | tf_op jit(solution)/shard_map/while/body/eval_jaxpr/ppermute | solution.py:14
  41.5 298.2 %collective-permute-start.1 = (bf16[128,576]{1,0:T(8,128)(2,1)S(1)}, bf16[128,576]{1,0:T(8,128)(2,1)S(1)}, u32[]{:S(2)}, u32[]{:S(2)}) collective-permute-start(bf16[128,576]{1,0:T(8,128)(2,1)S(1)} %get-tuple-element.176), channel_id=1, source_target_pairs={{0,4},{4,8},{8,12},{12,16},{16,20},{20,24},{24,28},{28,32},{32,36}... | collective-permute-start | bytes 442376 | tf_op jit(solution)/shard_map/while/body/eval_jaxpr/ppermute | solution.py:14
  42.7 300.0 %copy-start.1 = (f32[128,16,512]{2,0,1:T(8,128)S(1)}, f32[128,16,512]{2,0,1:T(8,128)}, u32[]{:S(2)}) copy-start(f32[128,16,512]{2,0,1:T(8,128)} %get-tuple-element.175) | copy-start | bytes 12582916 | tf_op jit(solution)/shard_map/while
  344.4 1.9 copy-start.2
  346.3 6.6 %collective-permute-start = (s32[128]{0:T(128)S(1)}, s32[128]{0:T(128)S(1)}, u32[]{:S(2)}, u32[]{:S(2)}) collective-permute-start(s32[128]{0:T(128)S(1)} %get-tuple-element.177), channel_id=1, source_target_pairs={{0,4},{4,8},{8,12},{12,16},{16,20},{20,24},{24,28},{28,32},{32,36}... | collective-permute-start | bytes 1544 | tf_op jit(solution)/shard_map/while/body/eval_jaxpr/ppermute | solution.py:14
  346.3 12.2 %collective-permute-start.1 = (bf16[128,576]{1,0:T(8,128)(2,1)S(1)}, bf16[128,576]{1,0:T(8,128)(2,1)S(1)}, u32[]{:S(2)}, u32[]{:S(2)}) collective-permute-start(bf16[128,576]{1,0:T(8,128)(2,1)S(1)} %get-tuple-element.176), channel_id=1, source_target_pairs={{0,4},{4,8},{8,12},{12,16},{16,20},{20,24},{24,28},{28,32},{32,36}... | collective-permute-start | bytes 442376 | tf_op jit(solution)/shard_map/while/body/eval_jaxpr/ppermute | solution.py:14
  346.4 15.2 %copy-start.1 = (f32[128,16,512]{2,0,1:T(8,128)S(1)}, f32[128,16,512]{2,0,1:T(8,128)}, u32[]{:S(2)}) copy-start(f32[128,16,512]{2,0,1:T(8,128)} %get-tuple-element.175) | copy-start | bytes 12582916 | tf_op jit(solution)/shard_map/while
  363.2 1.9 copy-start.2
  365.2 6.6 %collective-permute-start = (s32[128]{0:T(128)S(1)}, s32[128]{0:T(128)S(1)}, u32[]{:S(2)}, u32[]{:S(2)}) collective-permute-start(s32[128]{0:T(128)S(1)} %get-tuple-element.177), channel_id=1, source_target_pairs={{0,4},{4,8},{8,12},{12,16},{16,20},{20,24},{24,28},{28,32},{32,36}... | collective-permute-start | bytes 1544 | tf_op jit(solution)/shard_map/while/body/eval_jaxpr/ppermute | solution.py:14
  365.2 8.4 %collective-permute-start.1 = (bf16[128,576]{1,0:T(8,128)(2,1)S(1)}, bf16[128,576]{1,0:T(8,128)(2,1)S(1)}, u32[]{:S(2)}, u32[]{:S(2)}) collective-permute-start(bf16[128,576]{1,0:T(8,128)(2,1)S(1)} %get-tuple-element.176), channel_id=1, source_target_pairs={{0,4},{4,8},{8,12},{12,16},{16,20},{20,24},{24,28},{28,32},{32,36}... | collective-permute-start | bytes 442376 | tf_op jit(solution)/shard_map/while/body/eval_jaxpr/ppermute | solution.py:14
  365.2 11.4 %copy-start.1 = (f32[128,16,512]{2,0,1:T(8,128)S(1)}, f32[128,16,512]{2,0,1:T(8,128)}, u32[]{:S(2)}) copy-start(f32[128,16,512]{2,0,1:T(8,128)} %get-tuple-element.175) | copy-start | bytes 12582916 | tf_op jit(solution)/shard_map/while
  378.2 1.9 copy-start.2
  380.2 6.6 %collective-permute-start = (s32[128]{0:T(128)S(1)}, s32[128]{0:T(128)S(1)}, u32[]{:S(2)}, u32[]{:S(2)}) collective-permute-start(s32[128]{0:T(128)S(1)} %get-tuple-element.177), channel_id=1, source_target_pairs={{0,4},{4,8},{8,12},{12,16},{16,20},{20,24},{24,28},{28,32},{32,36}... | collective-permute-start | bytes 1544 | tf_op jit(solution)/shard_map/while/body/eval_jaxpr/ppermute | solution.py:14
  380.2 8.4 %collective-permute-start.1 = (bf16[128,576]{1,0:T(8,128)(2,1)S(1)}, bf16[128,576]{1,0:T(8,128)(2,1)S(1)}, u32[]{:S(2)}, u32[]{:S(2)}) collective-permute-start(bf16[128,576]{1,0:T(8,128)(2,1)S(1)} %get-tuple-element.176), channel_id=1, source_target_pairs={{0,4},{4,8},{8,12},{12,16},{16,20},{20,24},{24,28},{28,32},{32,36}... | collective-permute-start | bytes 442376 | tf_op jit(solution)/shard_map/while/body/eval_jaxpr/ppermute | solution.py:14
  380.2 11.4 %copy-start.1 = (f32[128,16,512]{2,0,1:T(8,128)S(1)}, f32[128,16,512]{2,0,1:T(8,128)}, u32[]{:S(2)}) copy-start(f32[128,16,512]{2,0,1:T(8,128)} %get-tuple-element.175) | copy-start | bytes 12582916 | tf_op jit(solution)/shard_map/while
  393.2 1.9 copy-start.2
  395.2 6.6 %collective-permute-start = (s32[128]{0:T(128)S(1)}, s32[128]{0:T(128)S(1)}, u32[]{:S(2)}, u32[]{:S(2)}) collective-permute-start(s32[128]{0:T(128)S(1)} %get-tuple-element.177), channel_id=1, source_target_pairs={{0,4},{4,8},{8,12},{12,16},{16,20},{20,24},{24,28},{28,32},{32,36}... | collective-permute-start | bytes 1544 | tf_op jit(solution)/shard_map/while/body/eval_jaxpr/ppermute | solution.py:14
  395.2 8.4 %collective-permute-start.1 = (bf16[128,576]{1,0:T(8,128)(2,1)S(1)}, bf16[128,576]{1,0:T(8,128)(2,1)S(1)}, u32[]{:S(2)}, u32[]{:S(2)}) collective-permute-start(bf16[128,576]{1,0:T(8,128)(2,1)S(1)} %get-tuple-element.176), channel_id=1, source_target_pairs={{0,4},{4,8},{8,12},{12,16},{16,20},{20,24},{24,28},{28,32},{32,36}... | collective-permute-start | bytes 442376 | tf_op jit(solution)/shard_map/while/body/eval_jaxpr/ppermute | solution.py:14
  395.2 11.4 %copy-start.1 = (f32[128,16,512]{2,0,1:T(8,128)S(1)}, f32[128,16,512]{2,0,1:T(8,128)}, u32[]{:S(2)}) copy-start(f32[128,16,512]{2,0,1:T(8,128)} %get-tuple-element.175) | copy-start | bytes 12582916 | tf_op jit(solution)/shard_map/while
  408.2 1.9 copy-start.2
  410.2 6.6 %collective-permute-start = (s32[128]{0:T(128)S(1)}, s32[128]{0:T(128)S(1)}, u32[]{:S(2)}, u32[]{:S(2)}) collective-permute-start(s32[128]{0:T(128)S(1)} %get-tuple-element.177), channel_id=1, source_target_pairs={{0,4},{4,8},{8,12},{12,16},{16,20},{20,24},{24,28},{28,32},{32,36}... | collective-permute-start | bytes 1544 | tf_op jit(solution)/shard_map/while/body/eval_jaxpr/ppermute | solution.py:14
  410.2 8.4 %collective-permute-start.1 = (bf16[128,576]{1,0:T(8,128)(2,1)S(1)}, bf16[128,576]{1,0:T(8,128)(2,1)S(1)}, u32[]{:S(2)}, u32[]{:S(2)}) collective-permute-start(bf16[128,576]{1,0:T(8,128)(2,1)S(1)} %get-tuple-element.176), channel_id=1, source_target_pairs={{0,4},{4,8},{8,12},{12,16},{16,20},{20,24},{24,28},{28,32},{32,36}... | collective-permute-start | bytes 442376 | tf_op jit(solution)/shard_map/while/body/eval_jaxpr/ppermute | solution.py:14
  410.2 11.4 %copy-start.1 = (f32[128,16,512]{2,0,1:T(8,128)S(1)}, f32[128,16,512]{2,0,1:T(8,128)}, u32[]{:S(2)}) copy-start(f32[128,16,512]{2,0,1:T(8,128)} %get-tuple-element.175) | copy-start | bytes 12582916 | tf_op jit(solution)/shard_map/while
  423.3 1.9 copy-start.2
  425.2 6.6 %collective-permute-start = (s32[128]{0:T(128)S(1)}, s32[128]{0:T(128)S(1)}, u32[]{:S(2)}, u32[]{:S(2)}) collective-permute-start(s32[128]{0:T(128)S(1)} %get-tuple-element.177), channel_id=1, source_target_pairs={{0,4},{4,8},{8,12},{12,16},{16,20},{20,24},{24,28},{28,32},{32,36}... | collective-permute-start | bytes 1544 | tf_op jit(solution)/shard_map/while/body/eval_jaxpr/ppermute | solution.py:14
  425.2 8.4 %collective-permute-start.1 = (bf16[128,576]{1,0:T(8,128)(2,1)S(1)}, bf16[128,576]{1,0:T(8,128)(2,1)S(1)}, u32[]{:S(2)}, u32[]{:S(2)}) collective-permute-start(bf16[128,576]{1,0:T(8,128)(2,1)S(1)} %get-tuple-element.176), channel_id=1, source_target_pairs={{0,4},{4,8},{8,12},{12,16},{16,20},{20,24},{24,28},{28,32},{32,36}... | collective-permute-start | bytes 442376 | tf_op jit(solution)/shard_map/while/body/eval_jaxpr/ppermute | solution.py:14
  425.2 11.4 %copy-start.1 = (f32[128,16,512]{2,0,1:T(8,128)S(1)}, f32[128,16,512]{2,0,1:T(8,128)}, u32[]{:S(2)}) copy-start(f32[128,16,512]{2,0,1:T(8,128)} %get-tuple-element.175) | copy-start | bytes 12582916 | tf_op jit(solution)/shard_map/while
  438.3 1.9 copy-start.2
  440.2 6.6 %collective-permute-start = (s32[128]{0:T(128)S(1)}, s32[128]{0:T(128)S(1)}, u32[]{:S(2)}, u32[]{:S(2)}) collective-permute-start(s32[128]{0:T(128)S(1)} %get-tuple-element.177), channel_id=1, source_target_pairs={{0,4},{4,8},{8,12},{12,16},{16,20},{20,24},{24,28},{28,32},{32,36}... | collective-permute-start | bytes 1544 | tf_op jit(solution)/shard_map/while/body/eval_jaxpr/ppermute | solution.py:14
  440.2 8.4 %collective-permute-start.1 = (bf16[128,576]{1,0:T(8,128)(2,1)S(1)}, bf16[128,576]{1,0:T(8,128)(2,1)S(1)}, u32[]{:S(2)}, u32[]{:S(2)}) collective-permute-start(bf16[128,576]{1,0:T(8,128)(2,1)S(1)} %get-tuple-element.176), channel_id=1, source_target_pairs={{0,4},{4,8},{8,12},{12,16},{16,20},{20,24},{24,28},{28,32},{32,36}... | collective-permute-start | bytes 442376 | tf_op jit(solution)/shard_map/while/body/eval_jaxpr/ppermute | solution.py:14
  440.2 11.4 %copy-start.1 = (f32[128,16,512]{2,0,1:T(8,128)S(1)}, f32[128,16,512]{2,0,1:T(8,128)}, u32[]{:S(2)}) copy-start(f32[128,16,512]{2,0,1:T(8,128)} %get-tuple-element.175) | copy-start | bytes 12582916 | tf_op jit(solution)/shard_map/while
  453.3 1.9 copy-start.2
  455.2 6.6 %collective-permute-start = (s32[128]{0:T(128)S(1)}, s32[128]{0:T(128)S(1)}, u32[]{:S(2)}, u32[]{:S(2)}) collective-permute-start(s32[128]{0:T(128)S(1)} %get-tuple-element.177), channel_id=1, source_target_pairs={{0,4},{4,8},{8,12},{12,16},{16,20},{20,24},{24,28},{28,32},{32,36}... | collective-permute-start | bytes 1544 | tf_op jit(solution)/shard_map/while/body/eval_jaxpr/ppermute | solution.py:14
  455.2 8.4 %collective-permute-start.1 = (bf16[128,576]{1,0:T(8,128)(2,1)S(1)}, bf16[128,576]{1,0:T(8,128)(2,1)S(1)}, u32[]{:S(2)}, u32[]{:S(2)}) collective-permute-start(bf16[128,576]{1,0:T(8,128)(2,1)S(1)} %get-tuple-element.176), channel_id=1, source_target_pairs={{0,4},{4,8},{8,12},{12,16},{16,20},{20,24},{24,28},{28,32},{32,36}... | collective-permute-start | bytes 442376 | tf_op jit(solution)/shard_map/while/body/eval_jaxpr/ppermute | solution.py:14
  455.2 11.4 %copy-start.1 = (f32[128,16,512]{2,0,1:T(8,128)S(1)}, f32[128,16,512]{2,0,1:T(8,128)}, u32[]{:S(2)}) copy-start(f32[128,16,512]{2,0,1:T(8,128)} %get-tuple-element.175) | copy-start | bytes 12582916 | tf_op jit(solution)/shard_map/while
  468.3 1.9 copy-start.2
  470.2 6.6 %collective-permute-start = (s32[128]{0:T(128)S(1)}, s32[128]{0:T(128)S(1)}, u32[]{:S(2)}, u32[]{:S(2)}) collective-permute-start(s32[128]{0:T(128)S(1)} %get-tuple-element.177), channel_id=1, source_target_pairs={{0,4},{4,8},{8,12},{12,16},{16,20},{20,24},{24,28},{28,32},{32,36}... | collective-permute-start | bytes 1544 | tf_op jit(solution)/shard_map/while/body/eval_jaxpr/ppermute | solution.py:14
  470.2 8.4 %collective-permute-start.1 = (bf16[128,576]{1,0:T(8,128)(2,1)S(1)}, bf16[128,576]{1,0:T(8,128)(2,1)S(1)}, u32[]{:S(2)}, u32[]{:S(2)}) collective-permute-start(bf16[128,576]{1,0:T(8,128)(2,1)S(1)} %get-tuple-element.176), channel_id=1, source_target_pairs={{0,4},{4,8},{8,12},{12,16},{16,20},{20,24},{24,28},{28,32},{32,36}... | collective-permute-start | bytes 442376 | tf_op jit(solution)/shard_map/while/body/eval_jaxpr/ppermute | solution.py:14
  470.2 11.4 %copy-start.1 = (f32[128,16,512]{2,0,1:T(8,128)S(1)}, f32[128,16,512]{2,0,1:T(8,128)}, u32[]{:S(2)}) copy-start(f32[128,16,512]{2,0,1:T(8,128)} %get-tuple-element.175) | copy-start | bytes 12582916 | tf_op jit(solution)/shard_map/while
  483.3 1.9 copy-start.2
  485.2 6.6 %collective-permute-start = (s32[128]{0:T(128)S(1)}, s32[128]{0:T(128)S(1)}, u32[]{:S(2)}, u32[]{:S(2)}) collective-permute-start(s32[128]{0:T(128)S(1)} %get-tuple-element.177), channel_id=1, source_target_pairs={{0,4},{4,8},{8,12},{12,16},{16,20},{20,24},{24,28},{28,32},{32,36}... | collective-permute-start | bytes 1544 | tf_op jit(solution)/shard_map/while/body/eval_jaxpr/ppermute | solution.py:14
  485.2 8.4 %collective-permute-start.1 = (bf16[128,576]{1,0:T(8,128)(2,1)S(1)}, bf16[128,576]{1,0:T(8,128)(2,1)S(1)}, u32[]{:S(2)}, u32[]{:S(2)}) collective-permute-start(bf16[128,576]{1,0:T(8,128)(2,1)S(1)} %get-tuple-element.176), channel_id=1, source_target_pairs={{0,4},{4,8},{8,12},{12,16},{16,20},{20,24},{24,28},{28,32},{32,36}... | collective-permute-start | bytes 442376 | tf_op jit(solution)/shard_map/while/body/eval_jaxpr/ppermute | solution.py:14
  485.2 11.4 %copy-start.1 = (f32[128,16,512]{2,0,1:T(8,128)S(1)}, f32[128,16,512]{2,0,1:T(8,128)}, u32[]{:S(2)}) copy-start(f32[128,16,512]{2,0,1:T(8,128)} %get-tuple-element.175) | copy-start | bytes 12582916 | tf_op jit(solution)/shard_map/while
  498.3 1.9 copy-start.2
  500.2 6.8 %collective-permute-start = (s32[128]{0:T(128)S(1)}, s32[128]{0:T(128)S(1)}, u32[]{:S(2)}, u32[]{:S(2)}) collective-permute-start(s32[128]{0:T(128)S(1)} %get-tuple-element.177), channel_id=1, source_target_pairs={{0,4},{4,8},{8,12},{12,16},{16,20},{20,24},{24,28},{28,32},{32,36}... | collective-permute-start | bytes 1544 | tf_op jit(solution)/shard_map/while/body/eval_jaxpr/ppermute | solution.py:14
  500.2 8.4 %collective-permute-start.1 = (bf16[128,576]{1,0:T(8,128)(2,1)S(1)}, bf16[128,576]{1,0:T(8,128)(2,1)S(1)}, u32[]{:S(2)}, u32[]{:S(2)}) collective-permute-start(bf16[128,576]{1,0:T(8,128)(2,1)S(1)} %get-tuple-element.176), channel_id=1, source_target_pairs={{0,4},{4,8},{8,12},{12,16},{16,20},{20,24},{24,28},{28,32},{32,36}... | collective-permute-start | bytes 442376 | tf_op jit(solution)/shard_map/while/body/eval_jaxpr/ppermute | solution.py:14
  500.2 11.4 %copy-start.1 = (f32[128,16,512]{2,0,1:T(8,128)S(1)}, f32[128,16,512]{2,0,1:T(8,128)}, u32[]{:S(2)}) copy-start(f32[128,16,512]{2,0,1:T(8,128)} %get-tuple-element.175) | copy-start | bytes 12582916 | tf_op jit(solution)/shard_map/while
  513.3 1.9 copy-start.2
  515.2 6.9 %collective-permute-start = (s32[128]{0:T(128)S(1)}, s32[128]{0:T(128)S(1)}, u32[]{:S(2)}, u32[]{:S(2)}) collective-permute-start(s32[128]{0:T(128)S(1)} %get-tuple-element.177), channel_id=1, source_target_pairs={{0,4},{4,8},{8,12},{12,16},{16,20},{20,24},{24,28},{28,32},{32,36}... | collective-permute-start | bytes 1544 | tf_op jit(solution)/shard_map/while/body/eval_jaxpr/ppermute | solution.py:14
  515.2 9.4 %collective-permute-start.1 = (bf16[128,576]{1,0:T(8,128)(2,1)S(1)}, bf16[128,576]{1,0:T(8,128)(2,1)S(1)}, u32[]{:S(2)}, u32[]{:S(2)}) collective-permute-start(bf16[128,576]{1,0:T(8,128)(2,1)S(1)} %get-tuple-element.176), channel_id=1, source_target_pairs={{0,4},{4,8},{8,12},{12,16},{16,20},{20,24},{24,28},{28,32},{32,36}... | collective-permute-start | bytes 442376 | tf_op jit(solution)/shard_map/while/body/eval_jaxpr/ppermute | solution.py:14
  515.2 12.4 %copy-start.1 = (f32[128,16,512]{2,0,1:T(8,128)S(1)}, f32[128,16,512]{2,0,1:T(8,128)}, u32[]{:S(2)}) copy-start(f32[128,16,512]{2,0,1:T(8,128)} %get-tuple-element.175) | copy-start | bytes 12582916 | tf_op jit(solution)/shard_map/while
  531.3 6.6 %collective-permute-start = (s32[128]{0:T(128)S(1)}, s32[128]{0:T(128)S(1)}, u32[]{:S(2)}, u32[]{:S(2)}) collective-permute-start(s32[128]{0:T(128)S(1)} %get-tuple-element.177), channel_id=1, source_target_pairs={{0,4},{4,8},{8,12},{12,16},{16,20},{20,24},{24,28},{28,32},{32,36}... | collective-permute-start | bytes 1544 | tf_op jit(solution)/shard_map/while/body/eval_jaxpr/ppermute | solution.py:14
  531.3 10.0 %collective-permute-start.1 = (bf16[128,576]{1,0:T(8,128)(2,1)S(1)}, bf16[128,576]{1,0:T(8,128)(2,1)S(1)}, u32[]{:S(2)}, u32[]{:S(2)}) collective-permute-start(bf16[128,576]{1,0:T(8,128)(2,1)S(1)} %get-tuple-element.176), channel_id=1, source_target_pairs={{0,4},{4,8},{8,12},{12,16},{16,20},{20,24},{24,28},{28,32},{32,36}... | collective-permute-start | bytes 442376 | tf_op jit(solution)/shard_map/while/body/eval_jaxpr/ppermute | solution.py:14
  531.3 13.0 %copy-start.1 = (f32[128,16,512]{2,0,1:T(8,128)S(1)}, f32[128,16,512]{2,0,1:T(8,128)}, u32[]{:S(2)}) copy-start(f32[128,16,512]{2,0,1:T(8,128)} %get-tuple-element.175) | copy-start | bytes 12582916 | tf_op jit(solution)/shard_map/while
  547.9 6.6 %collective-permute-start = (s32[128]{0:T(128)S(1)}, s32[128]{0:T(128)S(1)}, u32[]{:S(2)}, u32[]{:S(2)}) collective-permute-start(s32[128]{0:T(128)S(1)} %get-tuple-element.177), channel_id=1, source_target_pairs={{0,4},{4,8},{8,12},{12,16},{16,20},{20,24},{24,28},{28,32},{32,36}... | collective-permute-start | bytes 1544 | tf_op jit(solution)/shard_map/while/body/eval_jaxpr/ppermute | solution.py:14
  547.9 9.2 %collective-permute-start.1 = (bf16[128,576]{1,0:T(8,128)(2,1)S(1)}, bf16[128,576]{1,0:T(8,128)(2,1)S(1)}, u32[]{:S(2)}, u32[]{:S(2)}) collective-permute-start(bf16[128,576]{1,0:T(8,128)(2,1)S(1)} %get-tuple-element.176), channel_id=1, source_target_pairs={{0,4},{4,8},{8,12},{12,16},{16,20},{20,24},{24,28},{28,32},{32,36}... | collective-permute-start | bytes 442376 | tf_op jit(solution)/shard_map/while/body/eval_jaxpr/ppermute | solution.py:14
  547.9 12.1 %copy-start.1 = (f32[128,16,512]{2,0,1:T(8,128)S(1)}, f32[128,16,512]{2,0,1:T(8,128)}, u32[]{:S(2)}) copy-start(f32[128,16,512]{2,0,1:T(8,128)} %get-tuple-element.175) | copy-start | bytes 12582916 | tf_op jit(solution)/shard_map/while
  (3 other events, 5.8 us)
Sparse Core Ops, SparseCore 0:
  578.9 57.2 reduce-scatter.1
